TPU v7x, 128 devices: a whole 4x4x4 slice. The times are simulated.
128 devices in a mesh: space: 64 (over x, y, z), sub: 2 (over core).
Axes of the slice: x: 4, y: 4, z: 4, core: 2. Of those that a mesh axis runs over, the one named last changes fastest.
Arguments:
- mode_rows: float32 [256, 1048576], P(None, ('space', 'sub')), as said below
- snapshots: float32 [3, 64, 1048576], P(None, None, ('space', 'sub')), as said below
- probe_fields: float32 [128, 1048576], P(None, ('space', 'sub')), as said below
- core_factor: float32 [256, 256], replicated, as said below
Outputs:
- new_modes: float32 [256, 1048576], P(None, ('space', 'sub'))
- new_core: float32 [256, 256], replicated
- captured: float32 [3, 256, 320], replicated
Inputs may be any that keep to these rules, and one draw needn't show every extreme that they name: `mode_rows`: rows of full rank, entries of order one. `snapshots`: fields of order one. `probe_fields`: fields of order one. `core_factor`: lower triangular with a positive diagonal.
All inputs are finite; a program needn't handle non-finite values.
Results may differ from a plain program's by a relative error of at most 0.0003.
Values sent between devices are 32-bit elements; how exact they have to be, the bound alone decides.
A program may use at most 128 MiB of HBM per device.

v0:
```python
import jax
import jax.numpy as jnp
from jax import lax
from jax.sharding import PartitionSpec as P

TURNS = 2
PRECISE = lax.Precision.HIGHEST


def row_inner(left, right):
    return lax.dot_general(left, right, (((1,), (1,)), ((), ())), precision=PRECISE)


def matmul_high(left, right):
    return jnp.dot(left, right, precision=PRECISE)


def block_cholesky(matrix):
    order = matrix.shape[0]
    width = 64
    lowered = jnp.zeros((order, order), jnp.float32)
    for start in range(0, order, width):
        finish = start + width
        done_rows = lowered[start:finish, :start]
        diag_block = matrix[start:finish, start:finish] - matmul_high(done_rows, done_rows.T)
        diag_factor = jnp.linalg.cholesky(diag_block)
        lowered = lowered.at[start:finish, start:finish].set(diag_factor)
        if finish < order:
            below = matrix[finish:, start:finish] - matmul_high(
                lowered[finish:, :start], done_rows.T
            )
            panel = jax.scipy.linalg.solve_triangular(diag_factor, below.T, lower=True).T
            lowered = lowered.at[finish:, start:finish].set(panel)
    return lowered


def update_core(core_now, projected, factor, turn_count):
    rank_count = core_now.shape[0]
    batch_count = factor.shape[0]
    upper = jnp.concatenate([core_now, projected], axis=1)
    bottom = jnp.concatenate([jnp.zeros((batch_count, rank_count), jnp.float32), factor.T], axis=1)
    stacked = jnp.concatenate([upper, bottom], axis=0)
    squared = matmul_high(stacked, stacked.T)
    rotation = jnp.eye(rank_count + batch_count, rank_count, dtype=jnp.float32)
    for sweep_index in range(turn_count):
        rotation = matmul_high(squared, rotation)
        lowered = block_cholesky(matmul_high(rotation.T, rotation))
        rotation = jax.scipy.linalg.solve_triangular(lowered, rotation.T, lower=True).T
    fresh_core = block_cholesky(matmul_high(rotation.T, matmul_high(squared, rotation)))
    return (rotation, fresh_core)


def orthonormalize(residual, volume):
    gram_local = row_inner(residual, residual)
    factor = block_cholesky(lax.psum(gram_local, ("space", "sub")) * volume)
    orthogonal = jax.scipy.linalg.solve_triangular(factor, residual, lower=True)
    return (factor, orthogonal)


def body(mode_rows, snapshots, probe_fields, core_factor):
    local_rows = mode_rows.shape[1]
    batch_count = snapshots.shape[0]
    batch_width = snapshots.shape[1]
    volume = 1.0 / (local_rows * lax.axis_size("space") * lax.axis_size("sub"))
    window = jnp.concatenate(
        [snapshots.reshape(batch_count * batch_width, local_rows), probe_fields], axis=0
    )
    basis_now = mode_rows
    core_now = core_factor
    captured = []
    for batch_index in range(batch_count):
        incoming = snapshots[batch_index]
        projected = lax.psum(row_inner(basis_now, incoming), ("space", "sub")) * volume
        residual = incoming - matmul_high(projected.T, basis_now)
        factor, orthogonal = orthonormalize(residual, volume)
        rotation, core_now = update_core(core_now, projected, factor, TURNS)
        basis_now = matmul_high(rotation.T, jnp.concatenate([basis_now, orthogonal], axis=0))
        captured.append(lax.psum(row_inner(basis_now, window), ("space", "sub")) * volume)
    return (basis_now, core_now, jnp.stack(captured))


def solution(mesh):
    return jax.shard_map(
        body,
        mesh=mesh,
        in_specs=(
            P(None, ("space", "sub")),
            P(None, None, ("space", "sub")),
            P(None, ("space", "sub")),
            P(),
        ),
        out_specs=(P(None, ("space", "sub")), P(), P()),
        check_vma=False,
    )
```

profile of v0, /device:TPU:1, one launch (start us, length us, event | category | flops | bytes accessed | tf_op | source)
XLA Modules:
  0.0 1623.2 jit_solution(15675498892306487198)
XLA Ops:
  7.2 10.0 fusion.19
  17.3 143.2 %all-reduce.18.cloned.1.call-done = f32[256,64]{1,0:T(8,128)} async-done(((f32[256,64]{1,0:T(8,128)}), f32[256,64]{1,0:T(8,128)}) %all-reduce.18.cloned.1.call-update) | async-done | bytes 65552 | tf_op jit(solution)/shard_map/psum | solution.py:73
  160.5 9.2 convolution_subtract_fusion.2
  171.5 63.6 %psum.64 = f32[64,64]{0,1:T(8,128)S(1)} all-reduce(f32[64,64]{0,1:T(8,128)S(1)} %fusion.442), channel_id=1, replica_groups=mesh['space'=64,'sub'=2] {'space','sub'}, use_global_device_ids=true, to_apply=%region_1.0 | all-reduce | flops 4096 | bytes 32768 | tf_op jit(solution)/shard_map/psum | solution.py:55
  245.5 5.8 cholesky.610
  308.2 20.1 %custom-call.51 = f32[2,128,128]{1,2,0:T(8,128)S(1)} custom-call(f32[2,128,128]{2,1,0:T(8,128)S(1)} %get-tuple-element.863), custom_call_target="InvertDiagBlocksLowerTriangular" | custom-call | tf_op jit(solution)/shard_map/jit(_solve_triangular)/triangular_solve | solution.py:48
  330.9 5.8 cholesky.654
  398.1 19.8 %custom-call.55 = f32[2,128,128]{1,2,0:T(8,128)S(1)} custom-call(f32[2,128,128]{2,1,0:T(8,128)S(1)} %get-tuple-element.864), custom_call_target="InvertDiagBlocksLowerTriangular" | custom-call | tf_op jit(solution)/shard_map/jit(_solve_triangular)/triangular_solve | solution.py:48
  420.5 5.8 cholesky.698
  480.7 16.3 %fusion = f32[256,8192]{1,0:T(8,128)S(1)} fusion(f32[64,8192]{1,0:T(8,128)} %fusion.189, f32[256,8192]{1,0:T(8,128)} %param.153, f32[128,320]{0,1:T(8,128)S(1)} %fusion.125, f32[128,320]{0,1:T(8,128)S(1)} %fusion.98), kind=kOutput, calls=%fused_computation.12 | convolution fusion | flops 8055767040 | bytes 19202048 | tf_op jit(solution)/shard_map/dot_general | solution.py:15
  500.4 8.9 fusion.17
  509.3 13.3 fusion.14
  524.3 122.0 %all-reduce.20.cloned.1.call-done = f32[256,64]{1,0:T(8,128)} async-done(((f32[256,64]{1,0:T(8,128)}), f32[256,64]{1,0:T(8,128)}) %all-reduce.20.cloned.1.call-update) | async-done | bytes 65552 | tf_op jit(solution)/shard_map/psum | solution.py:73
  646.3 9.2 convolution_subtract_fusion.1
  657.2 63.7 %psum.66 = f32[64,64]{0,1:T(8,128)S(1)} all-reduce(f32[64,64]{0,1:T(8,128)S(1)} %fusion.445), channel_id=1, replica_groups=mesh['space'=64,'sub'=2] {'space','sub'}, use_global_device_ids=true, to_apply=%region_5.12 | all-reduce | flops 4096 | bytes 32768 | tf_op jit(solution)/shard_map/psum | solution.py:55
  731.3 5.8 cholesky.753
  794.5 19.8 %custom-call.63 = f32[2,128,128]{1,2,0:T(8,128)S(1)} custom-call(f32[2,128,128]{2,1,0:T(8,128)S(1)} %get-tuple-element.865), custom_call_target="InvertDiagBlocksLowerTriangular" | custom-call | tf_op jit(solution)/shard_map/jit(_solve_triangular)/triangular_solve | solution.py:48
  816.9 5.8 cholesky.797
  884.3 19.9 %custom-call.67 = f32[2,128,128]{1,2,0:T(8,128)S(1)} custom-call(f32[2,128,128]{2,1,0:T(8,128)S(1)} %get-tuple-element.866), custom_call_target="InvertDiagBlocksLowerTriangular" | custom-call | tf_op jit(solution)/shard_map/jit(_solve_triangular)/triangular_solve | solution.py:48
  906.7 5.8 cholesky.841
  944.9 17.2 %fusion.4 = f32[256,8192]{1,0:T(8,128)S(1)} fusion(f32[64,8192]{1,0:T(8,128)S(1)} %fusion.165, f32[256,8192]{1,0:T(8,128)} %copy-done.1, f32[128,320]{0,1:T(8,128)S(1)} %fusion.115, f32[128,320]{0,1:T(8,128)S(1)} %fusion.94), kind=kOutput, calls=%fused_computation.16 | convolution fusion | flops 8055767040 | bytes 19202048 | tf_op jit(solution)/shard_map/dot_general | solution.py:15
  965.3 8.9 fusion.15
  974.2 13.1 fusion.13
  1010.1 114.5 %all-reduce.22.cloned.1.call-done = f32[256,64]{1,0:T(8,128)} async-done(((f32[256,64]{1,0:T(8,128)}), f32[256,64]{1,0:T(8,128)}) %all-reduce.22.cloned.1.call-update) | async-done | bytes 65552 | tf_op jit(solution)/shard_map/psum | solution.py:73
  1124.6 9.2 convolution_subtract_fusion
  1135.6 63.8 %psum.68 = f32[64,64]{0,1:T(8,128)S(1)} all-reduce(f32[64,64]{0,1:T(8,128)S(1)} %fusion.448), channel_id=1, replica_groups=mesh['space'=64,'sub'=2] {'space','sub'}, use_global_device_ids=true, to_apply=%region_7.14 | all-reduce | flops 4096 | bytes 32768 | tf_op jit(solution)/shard_map/psum | solution.py:55
  1272.4 19.9 %custom-call.75 = f32[2,128,128]{1,2,0:T(8,128)S(1)} custom-call(f32[2,128,128]{2,1,0:T(8,128)S(1)} %get-tuple-element.867), custom_call_target="InvertDiagBlocksLowerTriangular" | custom-call | tf_op jit(solution)/shard_map/jit(_solve_triangular)/triangular_solve | solution.py:48
  1362.3 20.1 %custom-call.79 = f32[2,128,128]{1,2,0:T(8,128)S(1)} custom-call(f32[2,128,128]{2,1,0:T(8,128)S(1)} %get-tuple-element.868), custom_call_target="InvertDiagBlocksLowerTriangular" | custom-call | tf_op jit(solution)/shard_map/jit(_solve_triangular)/triangular_solve | solution.py:48
  1384.9 5.8 cholesky.984
  1422.8 18.3 %fusion.8 = f32[256,8192]{1,0:T(8,128)} fusion(f32[64,8192]{1,0:T(8,128)S(1)} %fusion.148, f32[256,8192]{1,0:T(8,128)} %copy-done, f32[128,320]{0,1:T(8,128)S(1)} %fusion.105, f32[128,320]{0,1:T(8,128)S(1)} %fusion.90), kind=kOutput, calls=%fused_computation.20 | convolution fusion | flops 8055767040 | bytes 19202048 | tf_op jit(solution)/shard_map/dot_general | solution.py:15
  1455.7 13.1 fusion.12
  1477.1 136.2 %all-reduce.24.cloned.1.call-done = (f32[256,320]{0,1:T(8,128)}, f32[256,320]{0,1:T(8,128)}, f32[256,320]{0,1:T(8,128)}) async-done(((f32[256,320]{0,1:T(8,128)}, f32[256,320]{0,1:T(8,128)}, f32[256,320]{0,1:T(8,128)}), (f32[256,320]{0,1:T(8,128)}, f32[256,320]{0,1:T(8,128)}, f32[256,320]{0,1:T(8,128)})) %all-reduce.24.cloned.1.call-update) | async-done | bytes 983056 | tf_op jit(solution)/shard_map/psum | solution.py:78
  (551 shorter events, 616.1 us)
Async XLA Ops:
  7.2 153.3 %all-reduce.18.cloned.1.call-start = ((), (), s32[]{:S(2)}) async-start(), calls=%async_computation | async-start | bytes 262144 | tf_op jit(solution)/shard_map/psum | solution.py:73
  17.2 629.1 %all-reduce.20.cloned.1.call-start = ((), (), s32[]{:S(2)}) async-start(), calls=%async_computation.1 | async-start | bytes 262144 | tf_op jit(solution)/shard_map/psum | solution.py:73
  17.3 225.8 %copy-start.9 = (f32[256,256]{1,0:T(8,128)S(1)}, f32[256,256]{1,0:T(8,128)}, u32[]{:S(2)}) copy-start(f32[256,256]{1,0:T(8,128)} %param.156) | copy-start | bytes 786436
  160.5 82.5 %copy-start.6 = (f32[256,64]{1,0:T(8,128)S(1)}, f32[256,64]{1,0:T(8,128)}, u32[]{:S(2)}) copy-start(f32[256,64]{1,0:T(8,128)} %all-reduce.18.cloned.1.call-done) | copy-start | bytes 196612
  245.4 34.5 %copy-start.2 = (f32[256,256]{0,1:T(8,128)}, f32[256,256]{0,1:T(8,128)S(1)}, u32[]{:S(2)}) copy-start(f32[256,256]{0,1:T(8,128)S(1)} %fusion.443) | copy-start | bytes 786436
  497.0 3.4 copy-start.1
  509.3 615.3 %all-reduce.22.cloned.1.call-start = ((), (), s32[]{:S(2)}) async-start(), calls=%async_computation.2 | async-start | bytes 262144 | tf_op jit(solution)/shard_map/psum | solution.py:73
  646.3 82.6 %copy-start.7 = (f32[256,64]{1,0:T(8,128)S(1)}, f32[256,64]{1,0:T(8,128)}, u32[]{:S(2)}) copy-start(f32[256,64]{1,0:T(8,128)} %all-reduce.20.cloned.1.call-done) | copy-start | bytes 196612
  731.2 34.8 %copy-start.3 = (f32[256,256]{0,1:T(8,128)}, f32[256,256]{0,1:T(8,128)S(1)}, u32[]{:S(2)}) copy-start(f32[256,256]{0,1:T(8,128)S(1)} %fusion.446) | copy-start | bytes 786436
  962.1 3.2 copy-start
  987.3 626.0 %all-reduce.24.cloned.1.call-start = ((), (), s32[]{:S(2)}) async-start(), calls=%async_computation.3 | async-start | bytes 1966080 | tf_op jit(solution)/shard_map/psum | solution.py:78
  1124.6 82.8 %copy-start.5 = (f32[256,64]{1,0:T(8,128)S(1)}, f32[256,64]{1,0:T(8,128)}, u32[]{:S(2)}) copy-start(f32[256,64]{1,0:T(8,128)} %all-reduce.22.cloned.1.call-done) | copy-start | bytes 196612
  1209.7 34.4 %copy-start.4 = (f32[256,256]{0,1:T(8,128)}, f32[256,256]{0,1:T(8,128)S(1)}, u32[]{:S(2)}) copy-start(f32[256,256]{0,1:T(8,128)S(1)} %fusion.449) | copy-start | bytes 786436
  1477.0 139.4 %copy-start.8 = (f32[256,256]{1,0:T(8,128)}, f32[256,256]{1,0:T(8,128)S(1)}, u32[]{:S(2)}) copy-start(f32[256,256]{1,0:T(8,128)S(1)} %scatter.314) | copy-start | bytes 786436
Sparse Core Ops, SparseCore 0:
  17.3 143.1 all-reduce.17
  509.4 136.8 all-reduce.19
  987.5 137.0 all-reduce.21
  1469.0 144.2 all-reduce.23
where the time goes:
time: 1630 us; the launch traced here: 1620 us
  other arithmetic  568 us (35%)
  waiting for transfers between devices  516 us (32%)
  matrix products  212 us (13%)
  blocking collectives  191 us (12%)
  local copies, waits for them, and re-layouts  118 us (7%)
  between operations  16.6 us (1%)
    psum x3, waiting for transfers between devices, body(): lax.psum(row_inner(basis_now, incoming), ('space', 'sub')) * volume  380 us
    another operation x117, other arithmetic, block_cholesky(): diag_factor = jnp.linalg.cholesky(diag_block)  255 us
    psum x3, blocking collectives, orthonormalize(): factor = block_cholesky(lax.psum(gram_local, ('space', 'sub')) * volume)  191 us
    another operation x54, other arithmetic, block_cholesky(): jax.scipy.linalg.solve_triangular(diag_factor, below.T, lower=True)  161 us
    psum x1, waiting for transfers between devices, body(): lax.psum(row_inner(basis_now, window), ('space', 'sub')) * volume  136 us
    another operation x13, other arithmetic, update_core(): jax.scipy.linalg.solve_triangular(lowered, rotation.T, lower=True)  123 us
    dot_general x72, matrix products, matmul_high(): return jnp.dot(left, right, precision=PRECISE)  114 us
    dot_general x9, matrix products, row_inner(): lax.dot_general(left, right, (((1,), (1,)), ((), ())), precision=PRECISE)  72.7 us
  transfers between devices with their start and end apart: 4, of which 4 were waited for; matrix products, arithmetic and copies ran while one was open for 3% of the time, Pallas kernels for 0%

commit v1 on v0

--- a/solution.py
+++ b/solution.py
@@ -5,6 +5,12 @@
 
 TURNS = 2
 PRECISE = lax.Precision.HIGHEST
+
+
+def write_outputs_by_axis(array_here, mesh_ax, mesh_dim):
+    for dd in (mesh_ax, mesh_dim):
+        array_here = lax.psum(array_here, dd)
+    return array_here
 
 
 def row_inner(left, right):
@@ -70,7 +76,7 @@
     captured = []
     for batch_index in range(batch_count):
         incoming = snapshots[batch_index]
-        projected = lax.psum(row_inner(basis_now, incoming), ("space", "sub")) * volume
+        projected = write_outputs_by_axis(row_inner(basis_now, incoming), "space", "sub") * volume
         residual = incoming - matmul_high(projected.T, basis_now)
         factor, orthogonal = orthonormalize(residual, volume)
         rotation, core_now = update_core(core_now, projected, factor, TURNS)

time: 1630 us -> 1660 us (1.018)
  waiting for transfers between devices: 516 us -> 536 us
    psum x3 -> x6, waiting for transfers between devices: 380 us -> 400 us  [write_outputs_by_axis(): array_here = lax.psum(array_here, dd)]
  transfers between devices with their start and end apart: 4 -> 7, of which waited for: 4 -> 7; matrix products, arithmetic and copies ran while one was open for 3% -> 3% of each run, Pallas kernels for 0% -> 0%
where the time goes in v1:
time: 1660 us; the launch traced here: 1650 us
  other arithmetic  568 us (34%)
  waiting for transfers between devices  536 us (32%)
  matrix products  212 us (13%)
  blocking collectives  201 us (12%)
  local copies, waits for them, and re-layouts  119 us (7%)
  between operations  16.9 us (1%)
    psum x6, waiting for transfers between devices, write_outputs_by_axis(): array_here = lax.psum(array_here, dd)  400 us
    another operation x117, other arithmetic, block_cholesky(): diag_factor = jnp.linalg.cholesky(diag_block)  255 us
    psum x3, blocking collectives, orthonormalize(): factor = block_cholesky(lax.psum(gram_local, ('space', 'sub')) * volume)  201 us
    another operation x54, other arithmetic, block_cholesky(): jax.scipy.linalg.solve_triangular(diag_factor, below.T, lower=True)  161 us
    psum x1, waiting for transfers between devices, body(): lax.psum(row_inner(basis_now, window), ('space', 'sub')) * volume  136 us
    another operation x13, other arithmetic, update_core(): jax.scipy.linalg.solve_triangular(lowered, rotation.T, lower=True)  123 us
    dot_general x72, matrix products, matmul_high(): return jnp.dot(left, right, precision=PRECISE)  114 us
    dot_general x9, matrix products, row_inner(): lax.dot_general(left, right, (((1,), (1,)), ((), ())), precision=PRECISE)  72.5 us
  transfers between devices with their start and end apart: 7, of which 7 were waited for; matrix products, arithmetic and copies ran while one was open for 3% of the time, Pallas kernels for 0%

profile of v1, /device:TPU:1, one launch (start us, length us, event | category | flops | bytes accessed | tf_op | source)
XLA Modules:
  0.0 1653.4 jit_solution(10292930476754275377)
XLA Ops:
  7.2 10.0 fusion.19
  17.2 124.4 %all-reduce.21.cloned.1.call-done = f32[256,64]{1,0:T(8,128)} async-done(((f32[256,64]{1,0:T(8,128)}), f32[256,64]{1,0:T(8,128)}) %all-reduce.21.cloned.1.call-update) | async-done | bytes 65552 | tf_op jit(solution)/shard_map/psum | solution.py:12
  141.8 26.2 %all-reduce.23.cloned.1.call-done = f32[256,64]{1,0:T(8,128)} async-done(((f32[256,64]{1,0:T(8,128)}), f32[256,64]{1,0:T(8,128)}) %all-reduce.23.cloned.1.call-update) | async-done | bytes 65552 | tf_op jit(solution)/shard_map/psum | solution.py:12
  167.9 9.2 convolution_subtract_fusion.2
  178.9 66.9 %psum.86 = f32[64,64]{0,1:T(8,128)S(1)} all-reduce(f32[64,64]{0,1:T(8,128)S(1)} %fusion.442), channel_id=1, replica_groups=mesh['space'=64,'sub'=2] {'space','sub'}, use_global_device_ids=true, to_apply=%region_2.0 | all-reduce | flops 4096 | bytes 32768 | tf_op jit(solution)/shard_map/psum | solution.py:61
  256.2 5.8 cholesky.610
  319.0 20.1 %custom-call.51 = f32[2,128,128]{1,2,0:T(8,128)S(1)} custom-call(f32[2,128,128]{2,1,0:T(8,128)S(1)} %get-tuple-element.863), custom_call_target="InvertDiagBlocksLowerTriangular" | custom-call | tf_op jit(solution)/shard_map/jit(_solve_triangular)/triangular_solve | solution.py:54
  341.6 5.8 cholesky.654
  408.8 19.8 %custom-call.55 = f32[2,128,128]{1,2,0:T(8,128)S(1)} custom-call(f32[2,128,128]{2,1,0:T(8,128)S(1)} %get-tuple-element.864), custom_call_target="InvertDiagBlocksLowerTriangular" | custom-call | tf_op jit(solution)/shard_map/jit(_solve_triangular)/triangular_solve | solution.py:54
  431.2 5.8 cholesky.698
  490.7 16.3 fusion
  510.4 8.9 fusion.17
  519.4 13.1 fusion.14
  533.2 103.9 %all-reduce.25.cloned.1.call-done = f32[256,64]{1,0:T(8,128)} async-done(((f32[256,64]{1,0:T(8,128)}), f32[256,64]{1,0:T(8,128)}) %all-reduce.25.cloned.1.call-update) | async-done | bytes 65552 | tf_op jit(solution)/shard_map/psum | solution.py:12
  639.0 24.1 %all-reduce.27.cloned.1.call-done = f32[256,64]{1,0:T(8,128)} async-done(((f32[256,64]{1,0:T(8,128)}), f32[256,64]{1,0:T(8,128)}) %all-reduce.27.cloned.1.call-update) | async-done | bytes 65552 | tf_op jit(solution)/shard_map/psum | solution.py:12
  663.1 9.2 convolution_subtract_fusion.1
  674.1 66.9 %psum.89 = f32[64,64]{0,1:T(8,128)S(1)} all-reduce(f32[64,64]{0,1:T(8,128)S(1)} %fusion.445), channel_id=1, replica_groups=mesh['space'=64,'sub'=2] {'space','sub'}, use_global_device_ids=true, to_apply=%region_7.14 | all-reduce | flops 4096 | bytes 32768 | tf_op jit(solution)/shard_map/psum | solution.py:61
  751.4 5.8 cholesky.753
  814.5 20.1 %custom-call.63 = f32[2,128,128]{1,2,0:T(8,128)S(1)} custom-call(f32[2,128,128]{2,1,0:T(8,128)S(1)} %get-tuple-element.865), custom_call_target="InvertDiagBlocksLowerTriangular" | custom-call | tf_op jit(solution)/shard_map/jit(_solve_triangular)/triangular_solve | solution.py:54
  904.6 19.8 %custom-call.67 = f32[2,128,128]{1,2,0:T(8,128)S(1)} custom-call(f32[2,128,128]{2,1,0:T(8,128)S(1)} %get-tuple-element.866), custom_call_target="InvertDiagBlocksLowerTriangular" | custom-call | tf_op jit(solution)/shard_map/jit(_solve_triangular)/triangular_solve | solution.py:54
  964.9 17.4 %fusion.4 = f32[256,8192]{1,0:T(8,128)S(1)} fusion(f32[64,8192]{1,0:T(8,128)S(1)} %fusion.165, f32[256,8192]{1,0:T(8,128)} %copy-done.1, f32[128,320]{0,1:T(8,128)S(1)} %fusion.115, f32[128,320]{0,1:T(8,128)S(1)} %fusion.94), kind=kOutput, calls=%fused_computation.16 | convolution fusion | flops 8055767040 | bytes 19202048 | tf_op jit(solution)/shard_map/dot_general | solution.py:21
  985.5 8.9 fusion.15
  994.5 13.1 fusion.13
  1028.7 96.8 %all-reduce.29.cloned.1.call-done = f32[256,64]{1,0:T(8,128)} async-done(((f32[256,64]{1,0:T(8,128)}), f32[256,64]{1,0:T(8,128)}) %all-reduce.29.cloned.1.call-update) | async-done | bytes 65552 | tf_op jit(solution)/shard_map/psum | solution.py:12
  1127.3 24.4 %all-reduce.31.cloned.1.call-done = f32[256,64]{1,0:T(8,128)} async-done(((f32[256,64]{1,0:T(8,128)}), f32[256,64]{1,0:T(8,128)}) %all-reduce.31.cloned.1.call-update) | async-done | bytes 65552 | tf_op jit(solution)/shard_map/psum | solution.py:12
  1151.7 9.2 convolution_subtract_fusion
  1162.7 66.9 %psum.92 = f32[64,64]{0,1:T(8,128)S(1)} all-reduce(f32[64,64]{0,1:T(8,128)S(1)} %fusion.448), channel_id=1, replica_groups=mesh['space'=64,'sub'=2] {'space','sub'}, use_global_device_ids=true, to_apply=%region_10.17 | all-reduce | flops 4096 | bytes 32768 | tf_op jit(solution)/shard_map/psum | solution.py:61
  1302.9 19.8 %custom-call.75 = f32[2,128,128]{1,2,0:T(8,128)S(1)} custom-call(f32[2,128,128]{2,1,0:T(8,128)S(1)} %get-tuple-element.867), custom_call_target="InvertDiagBlocksLowerTriangular" | custom-call | tf_op jit(solution)/shard_map/jit(_solve_triangular)/triangular_solve | solution.py:54
  1392.7 19.9 %custom-call.79 = f32[2,128,128]{1,2,0:T(8,128)S(1)} custom-call(f32[2,128,128]{2,1,0:T(8,128)S(1)} %get-tuple-element.868), custom_call_target="InvertDiagBlocksLowerTriangular" | custom-call | tf_op jit(solution)/shard_map/jit(_solve_triangular)/triangular_solve | solution.py:54
  1453.3 18.3 %fusion.8 = f32[256,8192]{1,0:T(8,128)} fusion(f32[64,8192]{1,0:T(8,128)S(1)} %fusion.148, f32[256,8192]{1,0:T(8,128)} %copy-done, f32[128,320]{0,1:T(8,128)S(1)} %fusion.105, f32[128,320]{0,1:T(8,128)S(1)} %fusion.90), kind=kOutput, calls=%fused_computation.20 | convolution fusion | flops 8055767040 | bytes 19202048 | tf_op jit(solution)/shard_map/dot_general | solution.py:21
  1486.1 13.1 fusion.12
  1507.5 135.8 %all-reduce.33.cloned.1.call-done = (f32[256,320]{0,1:T(8,128)}, f32[256,320]{0,1:T(8,128)}, f32[256,320]{0,1:T(8,128)}) async-done(((f32[256,320]{0,1:T(8,128)}, f32[256,320]{0,1:T(8,128)}, f32[256,320]{0,1:T(8,128)}), (f32[256,320]{0,1:T(8,128)}, f32[256,320]{0,1:T(8,128)}, f32[256,320]{0,1:T(8,128)})) %all-reduce.33.cloned.1.call-update) | async-done | bytes 983056 | tf_op jit(solution)/shard_map/psum | solution.py:84
  (560 shorter events, 634.0 us)
Async XLA Ops:
  7.2 134.5 %all-reduce.21.cloned.1.call-start = ((), (), s32[]{:S(2)}) async-start(), calls=%async_computation | async-start | bytes 262144 | tf_op jit(solution)/shard_map/psum | solution.py:12
  17.2 150.8 %all-reduce.23.cloned.1.call-start = ((), (), s32[]{:S(2)}) async-start(), calls=%async_computation.1 | async-start | bytes 262144 | tf_op jit(solution)/shard_map/psum | solution.py:12
  141.7 495.4 %all-reduce.25.cloned.1.call-start = ((), (), s32[]{:S(2)}) async-start(), calls=%async_computation.2 | async-start | bytes 262144 | tf_op jit(solution)/shard_map/psum | solution.py:12
  141.7 112.0 %copy-start.9 = (f32[256,256]{1,0:T(8,128)S(1)}, f32[256,256]{1,0:T(8,128)}, u32[]{:S(2)}) copy-start(f32[256,256]{1,0:T(8,128)} %param.156) | copy-start | bytes 786436
  167.9 85.8 %copy-start.7 = (f32[256,64]{1,0:T(8,128)S(1)}, f32[256,64]{1,0:T(8,128)}, u32[]{:S(2)}) copy-start(f32[256,64]{1,0:T(8,128)} %all-reduce.23.cloned.1.call-done) | copy-start | bytes 196612
  256.1 34.5 %copy-start.2 = (f32[256,256]{0,1:T(8,128)}, f32[256,256]{0,1:T(8,128)S(1)}, u32[]{:S(2)}) copy-start(f32[256,256]{0,1:T(8,128)S(1)} %fusion.443) | copy-start | bytes 786436
  507.0 3.4 copy-start.1
  519.4 143.8 %all-reduce.27.cloned.1.call-start = ((), (), s32[]{:S(2)}) async-start(), calls=%async_computation.3 | async-start | bytes 262144 | tf_op jit(solution)/shard_map/psum | solution.py:12
  637.1 488.4 %all-reduce.29.cloned.1.call-start = ((), (), s32[]{:S(2)}) async-start(), calls=%async_computation.4 | async-start | bytes 262144 | tf_op jit(solution)/shard_map/psum | solution.py:12
  663.1 85.8 %copy-start.5 = (f32[256,64]{1,0:T(8,128)S(1)}, f32[256,64]{1,0:T(8,128)}, u32[]{:S(2)}) copy-start(f32[256,64]{1,0:T(8,128)} %all-reduce.27.cloned.1.call-done) | copy-start | bytes 196612
  751.3 34.7 %copy-start.3 = (f32[256,256]{0,1:T(8,128)}, f32[256,256]{0,1:T(8,128)S(1)}, u32[]{:S(2)}) copy-start(f32[256,256]{0,1:T(8,128)S(1)} %fusion.446) | copy-start | bytes 786436
  982.3 3.2 copy-start
  1007.6 144.1 %all-reduce.31.cloned.1.call-start = ((), (), s32[]{:S(2)}) async-start(), calls=%async_computation.5 | async-start | bytes 262144 | tf_op jit(solution)/shard_map/psum | solution.py:12
  1125.6 517.7 %all-reduce.33.cloned.1.call-start = ((), (), s32[]{:S(2)}) async-start(), calls=%async_computation.6 | async-start | bytes 1966080 | tf_op jit(solution)/shard_map/psum | solution.py:84
  1151.7 85.8 %copy-start.6 = (f32[256,64]{1,0:T(8,128)S(1)}, f32[256,64]{1,0:T(8,128)}, u32[]{:S(2)}) copy-start(f32[256,64]{1,0:T(8,128)} %all-reduce.31.cloned.1.call-done) | copy-start | bytes 196612
  1239.9 34.6 %copy-start.4 = (f32[256,256]{0,1:T(8,128)}, f32[256,256]{0,1:T(8,128)S(1)}, u32[]{:S(2)}) copy-start(f32[256,256]{0,1:T(8,128)S(1)} %fusion.449) | copy-start | bytes 786436
  1507.4 138.9 %copy-start.8 = (f32[256,256]{1,0:T(8,128)}, f32[256,256]{1,0:T(8,128)S(1)}, u32[]{:S(2)}) copy-start(f32[256,256]{1,0:T(8,128)S(1)} %scatter.314) | copy-start | bytes 786436
Sparse Core Ops, SparseCore 0:
  17.3 124.3 all-reduce.20
  144.2 23.6 all-reduce.22
  519.5 117.5 all-reduce.24
  639.4 23.7 all-reduce.26
  1007.7 117.7 all-reduce.28
  1128.0 23.6 all-reduce.30
  1499.4 143.8 all-reduce.32
